TPU v7x, 32 devices: a whole 2x2x4 slice. The times are simulated.
32 devices in a mesh: blk: 8 (over z, x), pair: 4 (over y, core).
Axes of the slice: x: 2, y: 2, z: 4, core: 2. Of those that a mesh axis runs over, the one named last changes fastest.
Arguments:
- records: bfloat16 [8, 1024, 2048], P('blk', 'pair'), may hold values from -100 to 100
- offsets: int32 [2], replicated, may hold values from 1 to 7, as said below
- source_side: int32 [8, 2], P('blk'), may hold values from 0 to 1
Outputs:
- first_side: bfloat16 [8, 2, 32, 128, 128], P('blk', None, 'pair')
- second_side: bfloat16 [8, 2, 32, 128, 128], P('blk', None, 'pair')
Inputs may be any that keep to these rules, and one draw needn't show every extreme that they name: `offsets`: distinct and increasing; the last one is 7.
All inputs are finite; a program needn't handle non-finite values.
Results may differ from a plain program's by a relative error of at most 0.012.
Values may be sent and summed in bfloat16 or wider, within the bound.
No kernel may reach another device: no remote copies, remote signals or barrier semaphores. Data moves between devices by JAX's collectives and lax.ppermute only.
A program may use at most 128 MiB of HBM per device.

v0:
```python
import math
import jax
import jax.numpy as jnp
from jax import lax
from jax.sharding import PartitionSpec as P

BLOCK_CH = 128
BINS = 128
SAMPLES = 2048
FIRST_BIN = 4
LAGS = 32


def as_sent(value):
    return jax.tree.map(lambda a: a.astype(jnp.bfloat16) if a.dtype == jnp.float32 else a, value)


def shifted_2(value, axis, steps):
    count = lax.axis_size(axis)
    leading, last = (max(0, -steps), min(count, count - steps))
    return lax.ppermute(value, axis, [(source, source + steps) for source in range(leading, last)])


def fourier_table():
    sample_index = jnp.arange(SAMPLES, dtype=jnp.int32)
    bin_index = FIRST_BIN + jnp.arange(BINS, dtype=jnp.int32)
    phase_index = sample_index[:, None] * bin_index[None, :] % SAMPLES
    angles = 2.0 * math.pi / SAMPLES * phase_index.astype(jnp.float32)
    hann_taper = 0.5 - 0.5 * jnp.cos(2.0 * math.pi / SAMPLES * sample_index.astype(jnp.float32))
    return jnp.stack(
        (hann_taper[:, None] * jnp.cos(angles), -hann_taper[:, None] * jnp.sin(angles)), axis=-1
    )


def shift_ahead(distance):
    return lambda block: jax.tree.map(
        lambda part, own: part.astype(own.dtype), shifted_2(as_sent(block), "blk", -distance), block
    )


def local(records, offsets, source_side):
    seg_local = records.shape[0]
    local_blocks = records.shape[1] // BLOCK_CH
    table_full = fourier_table()
    table_high = lax.optimization_barrier(table_full.astype(jnp.bfloat16))
    table_low = (table_full - table_high.astype(jnp.float32)).astype(jnp.bfloat16)
    traces = records.reshape(seg_local, local_blocks, BLOCK_CH, SAMPLES)
    spectrum = jnp.einsum("sbcn,nfr->bfsrc", traces, table_high, preferred_element_type=jnp.float32)
    spectrum = spectrum + jnp.einsum(
        "sbcn,nfr->bfsrc", traces, table_low, preferred_element_type=jnp.float32
    )
    band_power = jnp.sum(spectrum * spectrum, axis=3)
    band_level = jnp.mean(band_power, axis=-1)
    whiten_scale = 1.0 / jnp.sqrt(band_level + 1e-05)
    whitened = (spectrum * whiten_scale[:, :, :, None, None]).astype(jnp.bfloat16)
    regrouped = lax.all_to_all(
        lax.all_to_all(whitened, "pair", split_axis=1, concat_axis=0, tiled=True),
        "blk",
        split_axis=0,
        concat_axis=2,
        tiled=True,
    )
    own_block = regrouped[0]
    bin_local = own_block.shape[0]
    seg_total = own_block.shape[1]
    offset_total = offsets.shape[0]
    group_size = lax.axis_size("blk")
    window_size = min(16, group_size)
    bit_total = window_size.bit_length() - 1
    ahead_list = [shift_ahead(distance) for distance in range(1, window_size)]
    partners = jnp.stack(
        [lax.switch(offsets[slot] - 1, ahead_list, own_block) for slot in range(offset_total)]
    )
    reverse_side = (source_side[0] == 1)[:, None, None, None, None]
    own_many = jnp.broadcast_to(own_block[None], partners.shape)
    source = jnp.where(reverse_side, partners, own_many)
    receiver = jnp.where(reverse_side, own_many, partners)
    left_side = source.reshape(offset_total, bin_local, 2 * seg_total, BLOCK_CH)
    rotated = jnp.stack((receiver[:, :, :, 1], -receiver[:, :, :, 0]), axis=3)
    right_side = jnp.stack((receiver, rotated), axis=4).reshape(
        offset_total, bin_local, 2 * seg_total, 2, BLOCK_CH
    )
    cross = jnp.einsum(
        "kfsc,kfsrd->kfrcd", left_side, right_side, preferred_element_type=jnp.float32
    )
    cross_rows = cross.reshape(offset_total, 2 * bin_local, BLOCK_CH * BLOCK_CH)
    pair_index = lax.axis_index("pair")
    lag_index = jnp.arange(LAGS, dtype=jnp.int32) - LAGS // 2
    bin_index = FIRST_BIN + pair_index * bin_local + jnp.arange(bin_local, dtype=jnp.int32)
    phase_index = lag_index[:, None] * bin_index[None, :] % SAMPLES
    angles = 2.0 * math.pi / SAMPLES * phase_index.astype(jnp.float32)
    normalizer = 1.0 / math.sqrt(seg_total * BINS)
    lag_table = (jnp.stack((jnp.cos(angles), -jnp.sin(angles)), axis=-1) * normalizer).reshape(
        LAGS, 2 * bin_local
    )
    summed = lax.psum_scatter(
        jnp.einsum(
            "lq,kqx->lkx",
            lag_table,
            cross_rows,
            precision=lax.Precision.HIGHEST,
            preferred_element_type=jnp.float32,
        ).astype(jnp.bfloat16),
        "pair",
        scatter_dimension=0,
        tiled=True,
    ).astype(jnp.float32)
    lag_local = summed.shape[0]
    first_local = (
        summed.astype(jnp.bfloat16)
        .transpose(1, 0, 2)
        .reshape(offset_total, lag_local, BLOCK_CH, BLOCK_CH)
    )
    returned = first_local
    for bit_number in range(bit_total):
        shifted = shifted_2(returned, "blk", 1 << bit_number)
        selected = (jnp.right_shift(offsets, bit_number) % 2 == 1)[:, None, None, None]
        returned = jnp.where(selected, shifted, returned)
    return (first_local[None], returned[None])


def solution(mesh):
    placed = (P("blk", "pair", None), P(), P("blk", None))
    return jax.shard_map(
        local,
        mesh=mesh,
        in_specs=placed,
        out_specs=(P("blk", None, "pair", None, None), P("blk", None, "pair", None, None)),
        check_vma=False,
    )
```

profile of v0, /device:TPU:25, one launch (start us, length us, event | category | flops | bytes accessed | tf_op | source)
XLA Modules:
  0.0 181.7 jit_solution(7638834543979147514)
XLA Ops:
  7.2 4.2 %cosine_multiply_fusion = (f32[2048,128,1]{1,0,2:T(8,128)S(1)}, f32[2048,128,1]{1,0,2:T(8,128)S(1)}) fusion(s32[128]{0:T(128)S(1)} %iota_add_fusion, f32[2048]{0:T(1024)S(1)} %get-tuple-element.57, f32[2048]{0:T(1024)S(1)} %get-tuple-element.58), kind=kLoop, calls=%fused_computation.18 | loop fusion | flops 4194304 | bytes 2114048 | tf_op jit(solution)/shard_map/mul | solution.py:31
  12.6 0.8 copy.65
  13.4 4.0 %all-to-all-start = ((bf16[2,128,1,2,128]{4,0,3,2,1:T(2,128)(2,1)}), bf16[2,128,1,2,128]{4,0,3,2,1:T(2,128)(2,1)S(1)}, u32[]{:S(2)}, u32[]{:S(2)}) async-start(bf16[2,128,1,2,128]{4,0,3,2,1:T(2,128)(2,1)} %copy.65), calls=%async_computation | async-start | bytes 262144 | tf_op jit(solution)/shard_map/all_to_all | solution.py:57
  17.6 3.4 %all-to-all-done = bf16[2,128,1,2,128]{4,0,3,2,1:T(2,128)(2,1)S(1)} async-done(((bf16[2,128,1,2,128]{4,0,3,2,1:T(2,128)(2,1)}), bf16[2,128,1,2,128]{4,0,3,2,1:T(2,128)(2,1)S(1)}, u32[]{:S(2)}, u32[]{:S(2)}) %all-to-all-start) | async-done | bytes 131104 | tf_op jit(solution)/shard_map/all_to_all | solution.py:57
  21.0 0.7 copy.67
  21.6 5.5 %all-to-all-start.1 = ((bf16[8,32,1,2,128]{4,1,3,2,0:T(8,128)(2,1)}), bf16[8,32,1,2,128]{4,1,3,2,0:T(8,128)(2,1)S(1)}, u32[]{:S(2)}, u32[]{:S(2)}) async-start(bf16[8,32,1,2,128]{4,1,3,2,0:T(8,128)(2,1)} %bitcast.15), calls=%async_computation.1 | async-start | bytes 262144 | tf_op jit(solution)/shard_map/all_to_all | solution.py:56
  27.1 0.6 fusion.36
  29.0 1.6 all-to-all-done.1
  30.7 4.9 %conditional.2 = (bf16[32,8,2,128]{3,2,1,0:T(2,128)(2,1)}) conditional(s32[]{:T(128)} %bitcast.19, bf16[32,8,2,128]{3,2,1,0:T(2,128)(2,1)S(1)} %copy.69, bf16[32,8,2,128]{3,2,1,0:T(2,128)(2,1)S(1)} %copy.69, bf16[32,8,2,128]{3,2,1,0:T(2,128)(2,1)S(1)} %copy.69, bf16[32,8,2,128]{3,2,1,0:T(2,128)(2,1)S(1)} %copy.69, ...), branch_computations={%region_1.2_spmd, %region_2.3_spmd, %region_3.4_spmd, %region_4.5_... | conditional | bytes 524336 | solution.py:72
  30.7 3.6 %collective-permute-start.1 = (bf16[32,8,2,128]{3,2,1,0:T(2,128)(2,1)S(1)}, bf16[32,8,2,128]{3,2,1,0:T(2,128)(2,1)}, u32[]{:S(2)}, u32[]{:S(2)}) collective-permute-start(bf16[32,8,2,128]{3,2,1,0:T(2,128)(2,1)S(1)} %param.1), channel_id=1, source_target_pairs={{8,0},{12,4},{16,8},{20,12},{24,16},{28,20},{9,1},{13,5},{17,9},{2... | collective-permute-start | bytes 393224 | tf_op jit(solution)/shard_map/cond/branch_1_fun/ppermute | solution.py:21
  34.3 1.3 collective-permute-done.1
  35.6 1.3 conditional.3
  35.6 1.3 collective-permute-start.13
  37.0 1.4 broadcast_select_fusion
  38.9 0.6 pad_maximum_fusion.1
  39.5 1.1 maximum_select_fusion
  40.6 5.5 %convolution_bitcast_fusion = f32[2,32,2,128,128]{3,4,2,1,0:T(8,128)} fusion(bf16[2,32,16,1,128]{4,2,3,1,0:T(8,128)(2,1)S(1)} %bitcast.79, bf16[2,32,16,1,128]{4,2,3,1,0:T(8,128)(2,1)S(1)} %maximum_select_fusion, bf16[1,32,16,128]{3,2,1,0:T(8,128)(2,1)} %bitcast.30, bf16[1,32,16,128]{3,2,1,0:T(8,128)(2,1)} %bitcast.29, ...), kind=kOutput, calls=%fused_computation.2 | convolution fusion | flops 67633152 | bytes 9306114 | tf_op jit(solution)/shard_map/kfsc,kfsrd->kfrcd/dot_general | solution.py:83
  46.1 8.9 %copy.85 = f32[2,32,2,128,128]{4,3,2,1,0:T(8,128)} copy(f32[2,32,2,128,128]{3,4,2,1,0:T(8,128)} %convolution_bitcast_fusion) | data formatting | bytes 16777216 | tf_op jit(solution)/shard_map/kfsc,kfsrd->kfrcd/transpose | solution.py:83
  55.0 9.4 %reshape.414 = f32[2,64,16384]{2,1,0:T(8,128)} reshape(f32[2,32,2,128,128]{4,3,2,1,0:T(8,128)} %copy.85) | data formatting | bytes 16777216 | tf_op jit(solution)/shard_map/reshape | solution.py:86
  64.4 6.4 %fusion = bf16[2,4,8,16384]{3,2,1,0:T(8,128)(2,1)S(1)} fusion(f32[32,64,1]{0,1,2:T(8,128)S(1)} %bitcast.81, f32[2,64,16384]{2,1,0:T(8,128)} %reshape.414), kind=kOutput, calls=%fused_computation.1 | convolution fusion | flops 806354944 | bytes 10493952 | tf_op jit(solution)/shard_map/lq,kqx->lkx/dot_general | solution.py:97
  70.9 1.5 copy.97
  72.4 42.0 %reduce-scatter.4.cloned.1.call-done = bf16[8,32768]{1,0:T(8,128)(2,1)} async-done(((bf16[32,32768]{1,0:T(8,128)(2,1)}), bf16[8,32768]{1,0:T(8,128)(2,1)}) %reduce-scatter.4.cloned.1.call-update) | async-done | bytes 524304
  114.4 1.2 copy.87
  115.6 3.1 %collective-permute-start.14 = (bf16[2,8,128,128]{3,2,1,0:T(8,128)(2,1)S(1)}, bf16[2,8,128,128]{3,2,1,0:T(8,128)(2,1)S(1)}, u32[]{:S(2)}, u32[]{:S(2)}) collective-permute-start(bf16[2,8,128,128]{3,2,1,0:T(8,128)(2,1)S(1)} %copy.87), channel_id=1, source_target_pairs={{0,4},{4,8},{8,12},{12,16},{16,20},{20,24},{24,28},{1,5},{5,9},{9,... | collective-permute-start | bytes 1572872 | tf_op jit(solution)/shard_map/ppermute | solution.py:21
  118.8 12.3 %collective-permute-done.14 = bf16[2,8,128,128]{3,2,1,0:T(8,128)(2,1)S(1)} collective-permute-done((bf16[2,8,128,128]{3,2,1,0:T(8,128)(2,1)S(1)}, bf16[2,8,128,128]{3,2,1,0:T(8,128)(2,1)S(1)}, u32[]{:S(2)}, u32[]{:S(2)}) %collective-permute-start.14) | collective-permute-done | bytes 524320 | tf_op jit(solution)/shard_map/ppermute | solution.py:21
  131.1 1.2 broadcast_select_fusion.1
  132.2 1.3 collective-permute-start.15
  133.5 12.4 %collective-permute-done.15 = bf16[2,8,128,128]{3,2,1,0:T(8,128)(2,1)S(1)} collective-permute-done((bf16[2,8,128,128]{3,2,1,0:T(8,128)(2,1)S(1)}, bf16[2,8,128,128]{3,2,1,0:T(8,128)(2,1)S(1)}, u32[]{:S(2)}, u32[]{:S(2)}) %collective-permute-start.15) | collective-permute-done | bytes 524320 | tf_op jit(solution)/shard_map/ppermute | solution.py:21
  146.0 1.3 collective-permute-start.16
  147.3 0.9 copy.89
  148.2 25.7 %collective-permute-done.16 = bf16[2,8,128,128]{3,2,1,0:T(8,128)(2,1)S(1)} collective-permute-done((bf16[2,8,128,128]{3,2,1,0:T(8,128)(2,1)S(1)}, bf16[2,8,128,128]{3,2,1,0:T(8,128)(2,1)S(1)}, u32[]{:S(2)}, u32[]{:S(2)}) %collective-permute-start.16) | collective-permute-done | bytes 524320 | tf_op jit(solution)/shard_map/ppermute | solution.py:21
  173.9 0.9 select_bitcast_fusion
  (29 shorter events, 2.3 us)
Async XLA Ops:
  7.2 4.4 %copy-start = (bf16[1,256,2048]{2,1,0:T(8,128)(2,1)S(1)}, bf16[1,256,2048]{2,1,0:T(8,128)(2,1)}, u32[]{:S(2)}) copy-start(bf16[1,256,2048]{2,1,0:T(8,128)(2,1)} %param.17) | copy-start | bytes 3145732
  11.6 15.5 %copy-start.2 = (s32[2]{0:T(128)S(1)}, s32[2]{0:T(128)}, u32[]{:S(2)}) copy-start(s32[2]{0:T(128)} %param.18) | copy-start | bytes 28
  11.6 17.4 %copy-start.3 = (s32[1,2]{1,0:T(1,128)S(1)}, s32[1,2]{1,0:T(1,128)}, u32[]{:S(2)}) copy-start(s32[1,2]{1,0:T(1,128)} %param.19) | copy-start | bytes 28
  13.4 7.5 %all-to-all-start = ((bf16[2,128,1,2,128]{4,0,3,2,1:T(2,128)(2,1)}), bf16[2,128,1,2,128]{4,0,3,2,1:T(2,128)(2,1)S(1)}, u32[]{:S(2)}, u32[]{:S(2)}) async-start(bf16[2,128,1,2,128]{4,0,3,2,1:T(2,128)(2,1)} %copy.65), calls=%async_computation | async-start | bytes 262144 | tf_op jit(solution)/shard_map/all_to_all | solution.py:57
  21.6 8.9 %all-to-all-start.1 = ((bf16[8,32,1,2,128]{4,1,3,2,0:T(8,128)(2,1)}), bf16[8,32,1,2,128]{4,1,3,2,0:T(8,128)(2,1)S(1)}, u32[]{:S(2)}, u32[]{:S(2)}) async-start(bf16[8,32,1,2,128]{4,1,3,2,0:T(8,128)(2,1)} %bitcast.15), calls=%async_computation.1 | async-start | bytes 262144 | tf_op jit(solution)/shard_map/all_to_all | solution.py:56
  27.1 87.3 %reduce-scatter.4.cloned.1.call-start = ((), (), s32[]{:S(2)}) async-start(), calls=%async_computation.3 | async-start | bytes 2621440
  30.7 4.9 %collective-permute-start.1 = (bf16[32,8,2,128]{3,2,1,0:T(2,128)(2,1)S(1)}, bf16[32,8,2,128]{3,2,1,0:T(2,128)(2,1)}, u32[]{:S(2)}, u32[]{:S(2)}) collective-permute-start(bf16[32,8,2,128]{3,2,1,0:T(2,128)(2,1)S(1)} %param.1), channel_id=1, source_target_pairs={{8,0},{12,4},{16,8},{20,12},{24,16},{28,20},{9,1},{13,5},{17,9},{2... | collective-permute-start | bytes 393224 | tf_op jit(solution)/shard_map/cond/branch_1_fun/ppermute | solution.py:21
  35.6 1.3 collective-permute-start.13
  114.4 32.9 %copy-start.1 = (bf16[8,32768]{1,0:T(8,128)(2,1)S(1)}, bf16[8,32768]{1,0:T(8,128)(2,1)}, u32[]{:S(2)}) copy-start(bf16[8,32768]{1,0:T(8,128)(2,1)} %reduce-scatter.4.cloned.1.call-done) | copy-start | bytes 1572868
  115.6 15.4 %collective-permute-start.14 = (bf16[2,8,128,128]{3,2,1,0:T(8,128)(2,1)S(1)}, bf16[2,8,128,128]{3,2,1,0:T(8,128)(2,1)S(1)}, u32[]{:S(2)}, u32[]{:S(2)}) collective-permute-start(bf16[2,8,128,128]{3,2,1,0:T(8,128)(2,1)S(1)} %copy.87), channel_id=1, source_target_pairs={{0,4},{4,8},{8,12},{12,16},{16,20},{20,24},{24,28},{1,5},{5,9},{9,... | collective-permute-start | bytes 1572872 | tf_op jit(solution)/shard_map/ppermute | solution.py:21
  132.2 13.7 %collective-permute-start.15 = (bf16[2,8,128,128]{3,2,1,0:T(8,128)(2,1)S(1)}, bf16[2,8,128,128]{3,2,1,0:T(8,128)(2,1)S(1)}, u32[]{:S(2)}, u32[]{:S(2)}) collective-permute-start(bf16[2,8,128,128]{3,2,1,0:T(8,128)(2,1)S(1)} %broadcast_select_fusion.1), channel_id=1, source_target_pairs={{0,8},{4,12},{8,16},{12,20},{16,24},{20,28},{1,9},{5,13},{9,17},{1... | collective-permute-start | bytes 1572872 | tf_op jit(solution)/shard_map/ppermute | solution.py:21
  146.0 27.9 %collective-permute-start.16 = (bf16[2,8,128,128]{3,2,1,0:T(8,128)(2,1)S(1)}, bf16[2,8,128,128]{3,2,1,0:T(8,128)(2,1)S(1)}, u32[]{:S(2)}, u32[]{:S(2)}) collective-permute-start(bf16[2,8,128,128]{3,2,1,0:T(8,128)(2,1)S(1)} %broadcast_select_fusion.2), channel_id=1, source_target_pairs={{0,16},{4,20},{8,24},{12,28},{1,17},{5,21},{9,25},{13,29},{2,18},{... | collective-permute-start | bytes 1572872 | tf_op jit(solution)/shard_map/ppermute | solution.py:21
Sparse Core Ops, SparseCore 0:
  72.5 41.8 reduce-scatter.3
where the time goes:
time: 183 us; the launch traced here: 182 us
  waiting for transfers between devices  98.6 us (54%)
  local copies, waits for them, and re-layouts  24.2 us (13%)
  starting transfers between devices  20 us (11%)
  between operations  15.4 us (8%)
  matrix products  12.9 us (7%)
  other arithmetic  10.4 us (6%)
    ppermute x5, waiting for transfers between devices, shifted_2(): lax.ppermute(value, axis, [(source, source + steps) for source in range(l...  51.6 us
    unnamed x2, waiting for transfers between devices  42 us
    ppermute x5, starting transfers between devices, shifted_2(): lax.ppermute(value, axis, [(source, source + steps) for source in range(l...  10.6 us
    reshape x1, local copies, waits for them, and re-layouts, local(): cross_rows = cross.reshape(offset_total, 2 * bin_local, BLOCK_CH * BLOCK_CH)  9.44 us
    transpose x1, local copies, waits for them, and re-layouts, local(): jnp.einsum('kfsc,kfsrd->kfrcd', left_side, right_side, preferred_element_...  8.89 us
    dot_general x1, matrix products, local(): jnp.einsum('lq,kqx->lkx', lag_table, cross_rows, precision=lax.Precision....  6.43 us
    dot_general x1, matrix products, local(): jnp.einsum('kfsc,kfsrd->kfrcd', left_side, right_side, preferred_element_...  5.54 us
    all_to_all x1, starting transfers between devices, local(): lax.all_to_all(lax.all_to_all(whitened, 'pair', split_axis=1, concat_axis...  5.46 us
  transfers between devices with their start and end apart: 8, of which 7 were waited for; matrix products, arithmetic and copies ran while one was open for 1% of the time, Pallas kernels for 0%

commit v1 on v0

--- a/solution.py
+++ b/solution.py
@@ -9,6 +9,18 @@
 SAMPLES = 2048
 FIRST_BIN = 4
 LAGS = 32
+
+
+def cut_along(x, dim, devices):
+    lengths = x.shape
+    pieces = x.reshape(*lengths[:dim], devices, lengths[dim] // devices, *lengths[dim + 1 :])
+    return jnp.moveaxis(pieces, dim, 0)
+
+
+def in_order(blocks, dim):
+    blocks = jnp.moveaxis(blocks, 0, dim)
+    dims = blocks.shape
+    return blocks.reshape(*dims[:dim], dims[dim] * dims[dim + 1], *dims[dim + 2 :])
 
 
 def as_sent(value):
@@ -53,13 +65,15 @@
     band_level = jnp.mean(band_power, axis=-1)
     whiten_scale = 1.0 / jnp.sqrt(band_level + 1e-05)
     whitened = (spectrum * whiten_scale[:, :, :, None, None]).astype(jnp.bfloat16)
-    regrouped = lax.all_to_all(
-        lax.all_to_all(whitened, "pair", split_axis=1, concat_axis=0, tiled=True),
-        "blk",
-        split_axis=0,
-        concat_axis=2,
-        tiled=True,
-    )
+    array = lax.all_to_all(whitened, "pair", split_axis=1, concat_axis=0, tiled=True)
+    length, place = (lax.axis_size("blk"), lax.axis_index("blk"))
+    blocks = cut_along(array, 0, length)
+    done = [blocks[place]]
+    for step in range(1, length):
+        sent = blocks[place ^ step]
+        done.append(lax.ppermute(sent, "blk", [(i, i ^ step) for i in range(length)]))
+    blocks = jnp.stack(done)[place ^ jnp.arange(length)]
+    regrouped = in_order(blocks, 2)
     own_block = regrouped[0]
     bin_local = own_block.shape[0]
     seg_total = own_block.shape[1]

time: 183 us -> 187 us (1.022)
  waiting for transfers between devices: 98.6 us -> 101 us
  starting transfers between devices: 20 us -> 22.2 us
    ppermute x0 -> x7, starting transfers between devices: none -> 9.23 us  [local(): lax.ppermute(sent, 'blk', [(i, i ^ step) for i in range(length)])]
    all_to_all x1 -> x0, starting transfers between devices: 5.46 us -> none  [local(): lax.all_to_all(lax.all_to_all(whitened, 'pair', split_axis=1, concat_axis...]
    unnamed x2, waiting for transfers between devices: 42 us -> 45.5 us
    ppermute x0 -> x7, waiting for transfers between devices: none -> 2.17 us  [local(): lax.ppermute(sent, 'blk', [(i, i ^ step) for i in range(length)])]
    all_to_all x1, waiting for transfers between devices: 3.39 us -> 1.43 us  [local(): lax.all_to_all(whitened, 'pair', split_axis=1, concat_axis=0, tiled=True)]
  transfers between devices with their start and end apart: 8 -> 14, of which waited for: 7 -> 8; matrix products, arithmetic and copies ran while one was open for 1% -> 1% of each run, Pallas kernels for 0% -> 0%
where the time goes in v1:
time: 187 us; the launch traced here: 186 us
  waiting for transfers between devices  101 us (54%)
  local copies, waits for them, and re-layouts  24.2 us (13%)
  starting transfers between devices  22.2 us (12%)
  between operations  15.5 us (8%)
  matrix products  12.9 us (7%)
  other arithmetic  10.4 us (6%)
    ppermute x5, waiting for transfers between devices, shifted_2(): lax.ppermute(value, axis, [(source, source + steps) for source in range(l...  51.6 us
    unnamed x2, waiting for transfers between devices  45.5 us
    reshape x1, local copies, waits for them, and re-layouts, local(): cross_rows = cross.reshape(offset_total, 2 * bin_local, BLOCK_CH * BLOCK_CH)  9.45 us
    ppermute x7, starting transfers between devices, local(): lax.ppermute(sent, 'blk', [(i, i ^ step) for i in range(length)])  9.23 us
    ppermute x5, starting transfers between devices, shifted_2(): lax.ppermute(value, axis, [(source, source + steps) for source in range(l...  8.96 us
    transpose x1, local copies, waits for them, and re-layouts, local(): jnp.einsum('kfsc,kfsrd->kfrcd', left_side, right_side, preferred_element_...  8.87 us
    dot_general x1, matrix products, local(): jnp.einsum('lq,kqx->lkx', lag_table, cross_rows, precision=lax.Precision....  6.43 us
    dot_general x1, matrix products, local(): jnp.einsum('kfsc,kfsrd->kfrcd', left_side, right_side, preferred_element_...  5.55 us
  transfers between devices with their start and end apart: 14, of which 8 were waited for; matrix products, arithmetic and copies ran while one was open for 1% of the time, Pallas kernels for 0%

profile of v1, /device:TPU:25, one launch (start us, length us, event | category | flops | bytes accessed | tf_op | source)
XLA Modules:
  0.0 186.0 jit_solution(10682119108997970406)
XLA Ops:
  7.2 4.2 %cosine_multiply_fusion = (f32[2048,128,1]{1,0,2:T(8,128)S(1)}, f32[2048,128,1]{1,0,2:T(8,128)S(1)}) fusion(s32[128]{0:T(128)S(1)} %iota_add_fusion, f32[2048]{0:T(1024)S(1)} %get-tuple-element.62, f32[2048]{0:T(1024)S(1)} %get-tuple-element.63), kind=kLoop, calls=%fused_computation.19 | loop fusion | flops 4194304 | bytes 2114048 | tf_op jit(solution)/shard_map/mul | solution.py:43
  13.4 4.0 %all-to-all-start = ((bf16[2,128,1,2,128]{4,0,3,2,1:T(2,128)(2,1)}), bf16[2,128,1,2,128]{4,0,3,2,1:T(2,128)(2,1)S(1)}, u32[]{:S(2)}, u32[]{:S(2)}) async-start(bf16[2,128,1,2,128]{4,0,3,2,1:T(2,128)(2,1)} %copy.60), calls=%async_computation | async-start | bytes 262144 | tf_op jit(solution)/shard_map/all_to_all | solution.py:68
  19.5 1.4 all-to-all-done
  21.0 1.3 collective-permute-start.14
  22.5 1.3 collective-permute-start.16
  23.8 3.2 %collective-permute-start.18 = (bf16[1,32,1,2,128]{4,1,3,2,0:T(8,128)(2,1)S(1)}, bf16[1,32,1,2,128]{4,1,3,2,0:T(8,128)(2,1)S(1)}, u32[]{:S(2)}, u32[]{:S(2)}) collective-permute-start(bf16[1,32,1,2,128]{4,1,3,2,0:T(8,128)(2,1)S(1)} %get-tuple-element.44), channel_id=1, source_target_pairs={{0,20},{4,16},{8,28},{12,24},{16,4},{20,0},{24,12},{28,8},{1,21},{... | collective-permute-start | bytes 49160 | tf_op jit(solution)/shard_map/ppermute | solution.py:74
  27.1 3.2 %collective-permute-start.20 = (bf16[1,32,1,2,128]{4,1,3,2,0:T(8,128)(2,1)S(1)}, bf16[1,32,1,2,128]{4,1,3,2,0:T(8,128)(2,1)S(1)}, u32[]{:S(2)}, u32[]{:S(2)}) collective-permute-start(bf16[1,32,1,2,128]{4,1,3,2,0:T(8,128)(2,1)S(1)} %get-tuple-element.42), channel_id=1, source_target_pairs={{0,28},{4,24},{8,20},{12,16},{16,12},{20,8},{24,4},{28,0},{1,29},{... | collective-permute-start | bytes 49160 | tf_op jit(solution)/shard_map/ppermute | solution.py:74
  30.3 1.1 collective-permute-done.19
  31.4 1.1 collective-permute-done.20
  33.2 3.3 %conditional.2 = (bf16[32,8,2,128]{3,2,1,0:T(2,128)(2,1)}) conditional(s32[]{:T(128)} %bitcast.36, bf16[32,8,2,128]{3,2,1,0:T(2,128)(2,1)S(1)} %copy.65, bf16[32,8,2,128]{3,2,1,0:T(2,128)(2,1)S(1)} %copy.65, bf16[32,8,2,128]{3,2,1,0:T(2,128)(2,1)S(1)} %copy.65, bf16[32,8,2,128]{3,2,1,0:T(2,128)(2,1)S(1)} %copy.65, ...), branch_computations={%region_1.2_spmd, %region_2.3_spmd, %region_3.4_spmd, %region_4.5_... | conditional | bytes 524336 | solution.py:86
  33.2 2.0 %collective-permute-start.1 = (bf16[32,8,2,128]{3,2,1,0:T(2,128)(2,1)S(1)}, bf16[32,8,2,128]{3,2,1,0:T(2,128)(2,1)}, u32[]{:S(2)}, u32[]{:S(2)}) collective-permute-start(bf16[32,8,2,128]{3,2,1,0:T(2,128)(2,1)S(1)} %param.1), channel_id=1, source_target_pairs={{8,0},{12,4},{16,8},{20,12},{24,16},{28,20},{9,1},{13,5},{17,9},{2... | collective-permute-start | bytes 393224 | tf_op jit(solution)/shard_map/cond/branch_1_fun/ppermute | solution.py:33
  35.2 1.3 collective-permute-done.1
  36.5 1.3 conditional.3
  36.5 1.3 collective-permute-start.13
  37.8 1.4 broadcast_select_fusion
  40.4 1.1 maximum_select_fusion
  41.4 5.5 %convolution_bitcast_fusion = f32[2,32,2,128,128]{3,4,2,1,0:T(8,128)} fusion(bf16[2,32,16,1,128]{4,2,3,1,0:T(8,128)(2,1)S(1)} %bitcast.112, bf16[2,32,16,1,128]{4,2,3,1,0:T(8,128)(2,1)S(1)} %maximum_select_fusion, bf16[1,32,16,128]{3,2,1,0:T(8,128)(2,1)} %bitcast.47, bf16[1,32,16,128]{3,2,1,0:T(8,128)(2,1)} %bitcast.46, ...), kind=kOutput, calls=%fused_computation.3 | convolution fusion | flops 67633152 | bytes 9306114 | tf_op jit(solution)/shard_map/kfsc,kfsrd->kfrcd/dot_general | solution.py:97
  47.0 8.9 %copy.81 = f32[2,32,2,128,128]{4,3,2,1,0:T(8,128)} copy(f32[2,32,2,128,128]{3,4,2,1,0:T(8,128)} %convolution_bitcast_fusion) | data formatting | bytes 16777216 | tf_op jit(solution)/shard_map/kfsc,kfsrd->kfrcd/transpose | solution.py:97
  55.9 9.4 %reshape.434 = f32[2,64,16384]{2,1,0:T(8,128)} reshape(f32[2,32,2,128,128]{4,3,2,1,0:T(8,128)} %copy.81) | data formatting | bytes 16777216 | tf_op jit(solution)/shard_map/reshape | solution.py:100
  65.3 6.4 %fusion = bf16[2,4,8,16384]{3,2,1,0:T(8,128)(2,1)S(1)} fusion(f32[32,64,1]{0,1,2:T(8,128)S(1)} %bitcast.117, f32[2,64,16384]{2,1,0:T(8,128)} %reshape.434), kind=kOutput, calls=%fused_computation.2 | convolution fusion | flops 806354944 | bytes 10493952 | tf_op jit(solution)/shard_map/lq,kqx->lkx/dot_general | solution.py:111
  71.8 1.5 copy.93
  73.3 45.5 %reduce-scatter.4.cloned.1.call-done = bf16[8,32768]{1,0:T(8,128)(2,1)} async-done(((bf16[32,32768]{1,0:T(8,128)(2,1)}), bf16[8,32768]{1,0:T(8,128)(2,1)}) %reduce-scatter.4.cloned.1.call-update) | async-done | bytes 524304
  118.8 1.2 copy.83
  120.0 3.1 %collective-permute-start.21 = (bf16[2,8,128,128]{3,2,1,0:T(8,128)(2,1)S(1)}, bf16[2,8,128,128]{3,2,1,0:T(8,128)(2,1)S(1)}, u32[]{:S(2)}, u32[]{:S(2)}) collective-permute-start(bf16[2,8,128,128]{3,2,1,0:T(8,128)(2,1)S(1)} %copy.83), channel_id=1, source_target_pairs={{0,4},{4,8},{8,12},{12,16},{16,20},{20,24},{24,28},{1,5},{5,9},{9,... | collective-permute-start | bytes 1572872 | tf_op jit(solution)/shard_map/ppermute | solution.py:33
  123.2 12.3 %collective-permute-done.21 = bf16[2,8,128,128]{3,2,1,0:T(8,128)(2,1)S(1)} collective-permute-done((bf16[2,8,128,128]{3,2,1,0:T(8,128)(2,1)S(1)}, bf16[2,8,128,128]{3,2,1,0:T(8,128)(2,1)S(1)}, u32[]{:S(2)}, u32[]{:S(2)}) %collective-permute-start.21) | collective-permute-done | bytes 524320 | tf_op jit(solution)/shard_map/ppermute | solution.py:33
  135.5 1.2 broadcast_select_fusion.1
  136.6 1.3 collective-permute-start.22
  137.9 12.4 %collective-permute-done.22 = bf16[2,8,128,128]{3,2,1,0:T(8,128)(2,1)S(1)} collective-permute-done((bf16[2,8,128,128]{3,2,1,0:T(8,128)(2,1)S(1)}, bf16[2,8,128,128]{3,2,1,0:T(8,128)(2,1)S(1)}, u32[]{:S(2)}, u32[]{:S(2)}) %collective-permute-start.22) | collective-permute-done | bytes 524320 | tf_op jit(solution)/shard_map/ppermute | solution.py:33
  150.4 1.3 collective-permute-start.23
  151.7 0.9 copy.85
  152.6 25.7 %collective-permute-done.23 = bf16[2,8,128,128]{3,2,1,0:T(8,128)(2,1)S(1)} collective-permute-done((bf16[2,8,128,128]{3,2,1,0:T(8,128)(2,1)S(1)}, bf16[2,8,128,128]{3,2,1,0:T(8,128)(2,1)S(1)}, u32[]{:S(2)}, u32[]{:S(2)}) %collective-permute-start.23) | collective-permute-done | bytes 524320 | tf_op jit(solution)/shard_map/ppermute | solution.py:33
  178.3 0.9 select_bitcast_fusion
  (53 shorter events, 5.2 us)
Async XLA Ops:
  7.2 4.4 %copy-start = (bf16[1,256,2048]{2,1,0:T(8,128)(2,1)S(1)}, bf16[1,256,2048]{2,1,0:T(8,128)(2,1)}, u32[]{:S(2)}) copy-start(bf16[1,256,2048]{2,1,0:T(8,128)(2,1)} %param.17) | copy-start | bytes 3145732
  11.6 5.8 %copy-start.2 = (s32[2]{0:T(128)S(1)}, s32[2]{0:T(128)}, u32[]{:S(2)}) copy-start(s32[2]{0:T(128)} %param.18) | copy-start | bytes 28
  11.6 7.6 %copy-start.3 = (s32[1,2]{1,0:T(1,128)S(1)}, s32[1,2]{1,0:T(1,128)}, u32[]{:S(2)}) copy-start(s32[1,2]{1,0:T(1,128)} %param.19) | copy-start | bytes 28
  13.4 7.5 %all-to-all-start = ((bf16[2,128,1,2,128]{4,0,3,2,1:T(2,128)(2,1)}), bf16[2,128,1,2,128]{4,0,3,2,1:T(2,128)(2,1)S(1)}, u32[]{:S(2)}, u32[]{:S(2)}) async-start(bf16[2,128,1,2,128]{4,0,3,2,1:T(2,128)(2,1)} %copy.60), calls=%async_computation | async-start | bytes 262144 | tf_op jit(solution)/shard_map/all_to_all | solution.py:68
  17.4 101.4 %reduce-scatter.4.cloned.1.call-start = ((), (), s32[]{:S(2)}) async-start(), calls=%async_computation.2 | async-start | bytes 2621440
  21.0 6.0 %collective-permute-start.14 = (bf16[1,32,1,2,128]{4,1,3,2,0:T(8,128)(2,1)S(1)}, bf16[1,32,1,2,128]{4,1,3,2,0:T(8,128)(2,1)S(1)}, u32[]{:S(2)}, u32[]{:S(2)}) collective-permute-start(bf16[1,32,1,2,128]{4,1,3,2,0:T(8,128)(2,1)S(1)} %get-tuple-element.48), channel_id=1, source_target_pairs={{0,4},{4,0},{8,12},{12,8},{16,20},{20,16},{24,28},{28,24},{1,5},{5... | collective-permute-start | bytes 49160 | tf_op jit(solution)/shard_map/ppermute | solution.py:74
  22.3 4.8 %collective-permute-start.15 = (bf16[1,32,1,2,128]{4,1,3,2,0:T(8,128)(2,1)S(1)}, bf16[1,32,1,2,128]{4,1,3,2,0:T(8,128)(2,1)S(1)}, u32[]{:S(2)}, u32[]{:S(2)}) collective-permute-start(bf16[1,32,1,2,128]{4,1,3,2,0:T(8,128)(2,1)S(1)} %get-tuple-element.47), channel_id=1, source_target_pairs={{0,8},{4,12},{8,0},{12,4},{16,24},{20,28},{24,16},{28,20},{1,9},{5... | collective-permute-start | bytes 49160 | tf_op jit(solution)/shard_map/ppermute | solution.py:74
  22.5 7.8 %collective-permute-start.16 = (bf16[1,32,1,2,128]{4,1,3,2,0:T(8,128)(2,1)S(1)}, bf16[1,32,1,2,128]{4,1,3,2,0:T(8,128)(2,1)S(1)}, u32[]{:S(2)}, u32[]{:S(2)}) collective-permute-start(bf16[1,32,1,2,128]{4,1,3,2,0:T(8,128)(2,1)S(1)} %get-tuple-element.46), channel_id=1, source_target_pairs={{0,12},{4,8},{8,4},{12,0},{16,28},{20,24},{24,20},{28,16},{1,13},{... | collective-permute-start | bytes 49160 | tf_op jit(solution)/shard_map/ppermute | solution.py:74
  23.7 6.6 %collective-permute-start.17 = (bf16[1,32,1,2,128]{4,1,3,2,0:T(8,128)(2,1)S(1)}, bf16[1,32,1,2,128]{4,1,3,2,0:T(8,128)(2,1)S(1)}, u32[]{:S(2)}, u32[]{:S(2)}) collective-permute-start(bf16[1,32,1,2,128]{4,1,3,2,0:T(8,128)(2,1)S(1)} %get-tuple-element.45), channel_id=1, source_target_pairs={{0,16},{4,20},{8,24},{12,28},{16,0},{20,4},{24,8},{28,12},{1,17},{... | collective-permute-start | bytes 49160 | tf_op jit(solution)/shard_map/ppermute | solution.py:74
  23.8 6.5 %collective-permute-start.18 = (bf16[1,32,1,2,128]{4,1,3,2,0:T(8,128)(2,1)S(1)}, bf16[1,32,1,2,128]{4,1,3,2,0:T(8,128)(2,1)S(1)}, u32[]{:S(2)}, u32[]{:S(2)}) collective-permute-start(bf16[1,32,1,2,128]{4,1,3,2,0:T(8,128)(2,1)S(1)} %get-tuple-element.44), channel_id=1, source_target_pairs={{0,20},{4,16},{8,28},{12,24},{16,4},{20,0},{24,12},{28,8},{1,21},{... | collective-permute-start | bytes 49160 | tf_op jit(solution)/shard_map/ppermute | solution.py:74
  27.0 4.4 %collective-permute-start.19 = (bf16[1,32,1,2,128]{4,1,3,2,0:T(8,128)(2,1)S(1)}, bf16[1,32,1,2,128]{4,1,3,2,0:T(8,128)(2,1)S(1)}, u32[]{:S(2)}, u32[]{:S(2)}) collective-permute-start(bf16[1,32,1,2,128]{4,1,3,2,0:T(8,128)(2,1)S(1)} %get-tuple-element.43), channel_id=1, source_target_pairs={{0,24},{4,28},{8,16},{12,20},{16,8},{20,12},{24,0},{28,4},{1,25},{... | collective-permute-start | bytes 49160 | tf_op jit(solution)/shard_map/ppermute | solution.py:74
  27.1 5.5 %collective-permute-start.20 = (bf16[1,32,1,2,128]{4,1,3,2,0:T(8,128)(2,1)S(1)}, bf16[1,32,1,2,128]{4,1,3,2,0:T(8,128)(2,1)S(1)}, u32[]{:S(2)}, u32[]{:S(2)}) collective-permute-start(bf16[1,32,1,2,128]{4,1,3,2,0:T(8,128)(2,1)S(1)} %get-tuple-element.42), channel_id=1, source_target_pairs={{0,28},{4,24},{8,20},{12,16},{16,12},{20,8},{24,4},{28,0},{1,29},{... | collective-permute-start | bytes 49160 | tf_op jit(solution)/shard_map/ppermute | solution.py:74
  33.2 3.2 %collective-permute-start.1 = (bf16[32,8,2,128]{3,2,1,0:T(2,128)(2,1)S(1)}, bf16[32,8,2,128]{3,2,1,0:T(2,128)(2,1)}, u32[]{:S(2)}, u32[]{:S(2)}) collective-permute-start(bf16[32,8,2,128]{3,2,1,0:T(2,128)(2,1)S(1)} %param.1), channel_id=1, source_target_pairs={{8,0},{12,4},{16,8},{20,12},{24,16},{28,20},{9,1},{13,5},{17,9},{2... | collective-permute-start | bytes 393224 | tf_op jit(solution)/shard_map/cond/branch_1_fun/ppermute | solution.py:33
  36.5 1.3 collective-permute-start.13
  118.8 32.9 %copy-start.1 = (bf16[8,32768]{1,0:T(8,128)(2,1)S(1)}, bf16[8,32768]{1,0:T(8,128)(2,1)}, u32[]{:S(2)}) copy-start(bf16[8,32768]{1,0:T(8,128)(2,1)} %reduce-scatter.4.cloned.1.call-done) | copy-start | bytes 1572868
  120.0 15.4 %collective-permute-start.21 = (bf16[2,8,128,128]{3,2,1,0:T(8,128)(2,1)S(1)}, bf16[2,8,128,128]{3,2,1,0:T(8,128)(2,1)S(1)}, u32[]{:S(2)}, u32[]{:S(2)}) collective-permute-start(bf16[2,8,128,128]{3,2,1,0:T(8,128)(2,1)S(1)} %copy.83), channel_id=1, source_target_pairs={{0,4},{4,8},{8,12},{12,16},{16,20},{20,24},{24,28},{1,5},{5,9},{9,... | collective-permute-start | bytes 1572872 | tf_op jit(solution)/shard_map/ppermute | solution.py:33
  136.6 13.7 %collective-permute-start.22 = (bf16[2,8,128,128]{3,2,1,0:T(8,128)(2,1)S(1)}, bf16[2,8,128,128]{3,2,1,0:T(8,128)(2,1)S(1)}, u32[]{:S(2)}, u32[]{:S(2)}) collective-permute-start(bf16[2,8,128,128]{3,2,1,0:T(8,128)(2,1)S(1)} %broadcast_select_fusion.1), channel_id=1, source_target_pairs={{0,8},{4,12},{8,16},{12,20},{16,24},{20,28},{1,9},{5,13},{9,17},{1... | collective-permute-start | bytes 1572872 | tf_op jit(solution)/shard_map/ppermute | solution.py:33
  150.4 27.9 %collective-permute-start.23 = (bf16[2,8,128,128]{3,2,1,0:T(8,128)(2,1)S(1)}, bf16[2,8,128,128]{3,2,1,0:T(8,128)(2,1)S(1)}, u32[]{:S(2)}, u32[]{:S(2)}) collective-permute-start(bf16[2,8,128,128]{3,2,1,0:T(8,128)(2,1)S(1)} %broadcast_select_fusion.2), channel_id=1, source_target_pairs={{0,16},{4,20},{8,24},{12,28},{1,17},{5,21},{9,25},{13,29},{2,18},{... | collective-permute-start | bytes 1572872 | tf_op jit(solution)/shard_map/ppermute | solution.py:33
Sparse Core Ops, SparseCore 0:
  73.4 45.3 reduce-scatter.3
